TPU v7x, 32 devices: a whole 2x2x4 slice. The times are simulated.
32 devices in a mesh: tm: 2 (over core), height: 16 (over z, y, x).
Axes of the slice: x: 2, y: 2, z: 4, core: 2. Of those that a mesh axis runs over, the one named last changes fastest.
Arguments:
- clip: bfloat16 [4, 128, 48, 256], P('tm', 'height'), may hold values from -6 to 6
- teacher: bfloat16 [4, 128, 48, 256], P('tm', 'height'), may hold values from -6 to 6
- kernel_one: bfloat16 [6912, 256], P('height'), may hold values from -0.078125 to 0.078125
- kernel_two: bfloat16 [6912, 256], P('height'), may hold values from -0.078125 to 0.078125
Outputs:
- student: bfloat16 [4, 128, 48, 256], P('tm', 'height')
- grad_one: float32 [6912, 256], P('height')
- grad_two: float32 [6912, 256], P('height')
All inputs are finite; a program needn't handle non-finite values.
Results may differ from a plain program's by a relative error of at most 0.013.
Values may be sent and summed in bfloat16 or wider, within the bound.
No kernel may reach another device: no remote copies, remote signals or barrier semaphores. Data moves between devices by JAX's collectives and lax.ppermute only.
A program may use at most 128 MiB of HBM per device.

v0:
```python
import math
import jax
import jax.numpy as jnp
from jax import lax
from jax.sharding import PartitionSpec as P


def shifted(value, axis, by):
    count = lax.axis_size(axis)
    pairs = [(i, i + by) for i in range(count) if 0 <= i + by < count]
    return lax.ppermute(value, axis, pairs)


def extended_2(cells, sides, width):
    for axis, dim in sides:
        count = lax.axis_size(axis)
        ends = count - 1
        head = lax.slice_in_dim(cells, 0, width, axis=dim)
        tail = lax.slice_in_dim(cells, cells.shape[dim] - width, cells.shape[dim], axis=dim)
        cells = jnp.concatenate(
            [
                lax.ppermute(tail, axis, [(i, (i + 1) % count) for i in range(ends)]),
                cells,
                lax.ppermute(head, axis, [((i + 1) % count, i) for i in range(ends)]),
            ],
            axis=dim,
        )
    return cells


def tap_offsets():
    return [(t_off, h_off, w_off) for t_off in range(3) for h_off in range(3) for w_off in range(3)]


def widen(stacked):
    return jnp.pad(stacked, ((0, 0), (0, 0), (1, 1), (0, 0)))


def clip_edges(rimmed):
    place = lax.axis_index("height")
    blocks = lax.axis_size("height")
    rows_n = rimmed.shape[1]
    row_ids = jnp.arange(rows_n, dtype=jnp.int32)
    cut = jnp.logical_or(
        jnp.logical_and(row_ids == 0, place == 0),
        jnp.logical_and(row_ids == rows_n - 1, place == blocks - 1),
    )
    return jnp.where(cut[None, :, None, None], jnp.zeros_like(rimmed), rimmed)


def causal_patches(values):
    frames_n, height_n, width_n, chans = values.shape
    earlier = shifted(values, "tm", 1)
    extended = jnp.concatenate([earlier, values], axis=0)
    rimmed = clip_edges(extended_2(extended, (("height", 1),), 1))
    padded = widen(rimmed)
    pieces = [
        padded[t_off : t_off + frames_n, h_off : h_off + height_n, w_off : w_off + width_n]
        for t_off, h_off, w_off in tap_offsets()
    ]
    return jnp.stack(pieces, axis=3).reshape(frames_n * height_n * width_n, 27 * chans)


def future_patches(grads):
    frames_n, height_n, width_n, chans = grads.shape
    later = shifted(grads, "tm", -1)
    extended = jnp.concatenate([grads, later], axis=0)
    rimmed = clip_edges(extended_2(extended, (("height", 1),), 1))
    padded = widen(rimmed)
    pieces = [
        padded[
            2 - t_off : 2 - t_off + frames_n,
            2 - h_off : 2 - h_off + height_n,
            2 - w_off : 2 - w_off + width_n,
        ]
        for t_off, h_off, w_off in tap_offsets()
    ]
    return jnp.stack(pieces, axis=3).reshape(frames_n * height_n * width_n, 27, chans)


def reduce_grad(local_grad):
    owned = lax.psum_scatter(
        local_grad.astype(jnp.bfloat16), "height", scatter_dimension=0, tiled=True
    )
    return lax.psum(owned, "tm").astype(jnp.float32)


def shards(clip, teacher, kernel_one, kernel_two):
    frames_n, height_n, width_n, chans = clip.shape
    full_one = lax.all_gather(kernel_one, "height", axis=0, tiled=True)
    patches_clip = causal_patches(clip)
    pre_act = jnp.dot(patches_clip, full_one, preferred_element_type=jnp.float32)
    hidden = jax.nn.silu(pre_act).astype(jnp.bfloat16)
    full_two = lax.all_gather(kernel_two, "height", axis=0, tiled=True)
    patches_hidden = causal_patches(hidden.reshape(frames_n, height_n, width_n, chans))
    branch = jnp.dot(patches_hidden, full_two, preferred_element_type=jnp.float32)
    output = clip.reshape(-1, chans).astype(jnp.float32) + branch
    count_all = frames_n * lax.axis_size("tm") * height_n * lax.axis_size("height") * width_n
    factor = 1.0 / math.sqrt(count_all)
    grad_out = ((output - teacher.reshape(-1, chans).astype(jnp.float32)) * factor).astype(
        jnp.bfloat16
    )
    contract_rows = (((0,), (0,)), ((), ()))
    grad_two = reduce_grad(
        lax.dot_general(patches_hidden, grad_out, contract_rows, preferred_element_type=jnp.float32)
    )
    grad_patches = future_patches(grad_out.reshape(frames_n, height_n, width_n, chans))
    grad_hidden = jnp.einsum(
        "rkc,kdc->rd",
        grad_patches,
        full_two.reshape(27, chans, chans),
        preferred_element_type=jnp.float32,
    )
    sigmoid_pre = jax.nn.sigmoid(pre_act)
    grad_pre = (grad_hidden * sigmoid_pre * (1.0 + pre_act * (1.0 - sigmoid_pre))).astype(
        jnp.bfloat16
    )
    grad_one = reduce_grad(
        lax.dot_general(patches_clip, grad_pre, contract_rows, preferred_element_type=jnp.float32)
    )
    student = output.astype(jnp.bfloat16).reshape(frames_n, height_n, width_n, chans)
    return (student, grad_one, grad_two)


def solution(mesh):
    in_specs = (
        P("tm", "height", None, None),
        P("tm", "height", None, None),
        P("height", None),
        P("height", None),
    )
    out_specs = (P("tm", "height", None, None), P("height", None), P("height", None))
    return jax.shard_map(shards, mesh=mesh, in_specs=in_specs, out_specs=out_specs, check_vma=False)
```

profile of v0, /device:TPU:0, one launch (start us, length us, event | category | flops | bytes accessed | tf_op | source)
XLA Modules:
  0.0 475.6 jit_solution(719828073563204116)
XLA Ops:
  7.9 2.4 collective-permute-start
  10.5 1.4 collective-permute-done
  13.0 4.2 collective-permute-start.1
  17.2 1.3 collective-permute-start.2
  18.5 1.3 collective-permute-done.1
  19.8 4.1 collective-permute-done.2
  26.5 23.9 %copy.7 = bf16[2,8,48,27,256]{4,3,2,1,0:T(8,128)(2,1)S(1)} copy(bf16[2,8,48,27,256]{4,2,1,0,3:T(8,128)(2,1)S(1)} %bitcast_dynamic-update-slice_fusion.18) | data formatting | bytes 21233664 | tf_op jit(solution)/shard_map/stack | solution.py:61
  50.4 10.2 %copy.9 = bf16[96,8,27,256]{3,1,2,0:T(8,128)(2,1)} copy(bf16[96,8,27,256]{3,2,1,0:T(8,128)(2,1)S(1)} %bitcast.205) | data formatting | bytes 21233664
  60.6 23.9 %all-gather.3.cloned.1.call-done = bf16[6912,256]{1,0:T(8,128)(2,1)} async-done(((bf16[432,256]{1,0:T(8,128)(2,1)}), bf16[6912,256]{1,0:T(8,128)(2,1)}) %all-gather.3.cloned.1.call-update) | async-done | bytes 3538960 | tf_op jit(solution)/shard_map/all_gather | solution.py:90
  84.5 8.8 %multiply_convert_fusion = (bf16[768,256]{1,0:T(8,128)(2,1)S(1)}, f32[768,256]{1,0:T(8,128)}) fusion(bf16[768,6912]{1,0:T(8,128)(2,1)} %bitcast.207, bf16[6912,256]{1,0:T(8,128)(2,1)} %all-gather.3.cloned.1.call-done), kind=kOutput, calls=%fused_computation.16 | convolution fusion | flops 2718892032 | bytes 15335424 | tf_op jit(solution)/shard_map/dot_general | solution.py:92
  93.3 1.3 collective-permute-start.3
  94.6 1.3 collective-permute-done.3
  95.9 3.4 collective-permute-start.4
  99.3 1.5 collective-permute-start.5
  101.8 4.1 collective-permute-done.5
  108.6 23.9 %copy.8 = bf16[2,8,48,27,256]{4,3,2,1,0:T(8,128)(2,1)S(1)} copy(bf16[2,8,48,27,256]{4,2,1,0,3:T(8,128)(2,1)S(1)} %bitcast_dynamic-update-slice_fusion) | data formatting | bytes 21233664 | tf_op jit(solution)/shard_map/stack | solution.py:61
  132.5 10.2 %copy.10 = bf16[96,8,27,256]{3,1,2,0:T(8,128)(2,1)} copy(bf16[96,8,27,256]{3,2,1,0:T(8,128)(2,1)S(1)} %bitcast.206) | data formatting | bytes 21233664
  142.7 14.7 %all-gather.5.cloned.1.call-done = bf16[6912,256]{1,0:T(8,128)(2,1)} async-done(((bf16[432,256]{1,0:T(8,128)(2,1)}), bf16[6912,256]{1,0:T(8,128)(2,1)}) %all-gather.5.cloned.1.call-update) | async-done | bytes 3538960 | tf_op jit(solution)/shard_map/all_gather | solution.py:94
  157.4 8.8 %fusion.4 = (bf16[768,256]{1,0:T(8,128)(2,1)S(1)}, bf16[768,256]{1,0:T(8,128)(2,1)}) fusion(bf16[2,8,48,256]{3,2,1,0:T(8,128)(2,1)S(1)} %copy-done.2, bf16[768,6912]{1,0:T(8,128)(2,1)} %bitcast.209, bf16[6912,256]{1,0:T(8,128)(2,1)} %all-gather.5.cloned.1.call-done, bf16[768,256]{1,0:T(8,128)(2,1)S(1)} %bitcast.246), kind=kOutput, calls=%fused_computation.12 | convolution fusion | flops 2719285248 | bytes 15728640 | tf_op jit(solution)/shard_map/dot_general | solution.py:96
  166.2 1.3 collective-permute-start.6
  167.6 4.5 convolution_convert_fusion
  172.2 3.4 collective-permute-start.7
  175.5 1.5 collective-permute-start.8
  177.0 1.5 collective-permute-done.7
  178.5 6.1 %collective-permute-done.8 = bf16[4,1,48,256]{3,2,1,0:T(8,128)(2,1)S(1)} collective-permute-done((bf16[4,1,48,256]{3,2,1,0:T(8,128)(2,1)S(1)}, bf16[4,1,48,256]{3,2,1,0:T(8,128)(2,1)S(1)}, u32[]{:S(2)}, u32[]{:S(2)}) %collective-permute-start.8) | collective-permute-done | bytes 98336 | tf_op jit(solution)/shard_map/ppermute | solution.py:24
  186.6 4.0 pad_slice_fusion
  210.2 20.4 %convolution_convert_fusion.1 = bf16[6912,256]{1,0:T(8,128)(2,1)} fusion(bf16[768,6912]{1,0:T(8,128)(2,1)} %bitcast.208, bf16[768,27,256]{2,0,1:T(8,128)(2,1)} %constant_dynamic-update-slice_fusion.2, bf16[27,256,256]{2,1,0:T(8,128)(2,1)S(1)} %bitcast.247, f32[768,256]{1,0:T(8,128)} %get-tuple-element.41), kind=kOutput, calls=%fused_computation.1 | convolution fusion | flops 5439356928 | bytes 29097984 | tf_op jit(solution)/shard_map/dot_general | solution.py:119
  230.6 75.9 %reduce-scatter.5.cloned.1.call-done = bf16[432,256]{1,0:T(8,128)(2,1)} async-done(((bf16[6912,256]{1,0:T(8,128)(2,1)}), bf16[432,256]{1,0:T(8,128)(2,1)}) %reduce-scatter.5.cloned.1.call-update) | async-done | bytes 221200 | tf_op jit(solution)/shard_map/reduce_scatter | solution.py:82
  306.6 139.2 %reduce-scatter.3.cloned.1.call-done = bf16[432,256]{1,0:T(8,128)(2,1)} async-done(((bf16[6912,256]{1,0:T(8,128)(2,1)}), bf16[432,256]{1,0:T(8,128)(2,1)}) %reduce-scatter.3.cloned.1.call-update) | async-done | bytes 221200 | tf_op jit(solution)/shard_map/reduce_scatter | solution.py:82
  445.8 19.8 %all-reduce.6.cloned.1.call-done = (bf16[432,256]{1,0:T(8,128)(2,1)}, bf16[432,256]{1,0:T(8,128)(2,1)}) async-done(((bf16[432,256]{1,0:T(8,128)(2,1)}, bf16[432,256]{1,0:T(8,128)(2,1)}), (bf16[432,256]{1,0:T(8,128)(2,1)}, bf16[432,256]{1,0:T(8,128)(2,1)})) %all-reduce.6.cloned.1.call-update) | async-done | bytes 442384 | tf_op jit(solution)/shard_map/psum | solution.py:85
  465.6 1.7 convert_element_type.49
  467.3 1.7 convert_element_type.51
  (116 shorter events, 29.7 us)
Async XLA Ops:
  7.2 77.3 %all-gather.3.cloned.1.call-start = ((), (), s32[]{:S(2)}) async-start(), calls=%async_computation.2 | async-start | bytes 3760128 | tf_op jit(solution)/shard_map/all_gather | solution.py:90
  7.9 149.5 %all-gather.5.cloned.1.call-start = ((), (), s32[]{:S(2)}) async-start(), calls=%async_computation.3 | async-start | bytes 3760128 | tf_op jit(solution)/shard_map/all_gather | solution.py:94
  7.9 3.9 collective-permute-start
  10.4 296.2 %reduce-scatter.5.cloned.1.call-start = ((), (), s32[]{:S(2)}) async-start(), calls=%async_computation.5 | async-start | bytes 3760128 | tf_op jit(solution)/shard_map/reduce_scatter | solution.py:82
  13.0 6.8 %collective-permute-start.1 = (bf16[4,1,48,256]{3,2,1,0:T(8,128)(2,1)S(1)}, bf16[4,1,48,256]{3,2,1,0:T(8,128)(2,1)S(1)}, u32[]{:S(2)}, u32[]{:S(2)}) collective-permute-start(bf16[4,1,48,256]{3,2,1,0:T(8,128)(2,1)S(1)} %get-tuple-element.38), channel_id=1, source_target_pairs={{0,1},{1,2},{2,3},{3,4},{4,5},{5,6},{6,7},{7,8},{8,9},{9,10},{10,1... | collective-permute-start | bytes 294920 | tf_op jit(solution)/shard_map/ppermute | solution.py:22
  17.2 6.7 %collective-permute-start.2 = (bf16[4,1,48,256]{3,2,1,0:T(8,128)(2,1)S(1)}, bf16[4,1,48,256]{3,2,1,0:T(8,128)(2,1)S(1)}, u32[]{:S(2)}, u32[]{:S(2)}) collective-permute-start(bf16[4,1,48,256]{3,2,1,0:T(8,128)(2,1)S(1)} %get-tuple-element.39), channel_id=1, source_target_pairs={{1,0},{2,1},{3,2},{4,3},{5,4},{6,5},{7,6},{8,7},{9,8},{10,9},{11,1... | collective-permute-start | bytes 294920 | tf_op jit(solution)/shard_map/ppermute | solution.py:24
  93.3 2.6 collective-permute-start.3
  95.9 5.9 %collective-permute-start.4 = (bf16[4,1,48,256]{3,2,1,0:T(8,128)(2,1)S(1)}, bf16[4,1,48,256]{3,2,1,0:T(8,128)(2,1)S(1)}, u32[]{:S(2)}, u32[]{:S(2)}) collective-permute-start(bf16[4,1,48,256]{3,2,1,0:T(8,128)(2,1)S(1)} %get-tuple-element.36), channel_id=1, source_target_pairs={{0,1},{1,2},{2,3},{3,4},{4,5},{5,6},{6,7},{7,8},{8,9},{9,10},{10,1... | collective-permute-start | bytes 294920 | tf_op jit(solution)/shard_map/ppermute | solution.py:22
  99.3 6.7 %collective-permute-start.5 = (bf16[4,1,48,256]{3,2,1,0:T(8,128)(2,1)S(1)}, bf16[4,1,48,256]{3,2,1,0:T(8,128)(2,1)S(1)}, u32[]{:S(2)}, u32[]{:S(2)}) collective-permute-start(bf16[4,1,48,256]{3,2,1,0:T(8,128)(2,1)S(1)} %get-tuple-element.37), channel_id=1, source_target_pairs={{1,0},{2,1},{3,2},{4,3},{5,4},{6,5},{7,6},{8,7},{9,8},{10,9},{11,1... | collective-permute-start | bytes 294920 | tf_op jit(solution)/shard_map/ppermute | solution.py:24
  132.5 24.9 %copy-start = (bf16[2,8,48,256]{3,2,1,0:T(8,128)(2,1)S(1)}, bf16[2,8,48,256]{3,2,1,0:T(8,128)(2,1)}, u32[]{:S(2)}) copy-start(bf16[2,8,48,256]{3,2,1,0:T(8,128)(2,1)} %param.4) | copy-start | bytes 1179652
  132.5 24.9 %copy-start.2 = (bf16[2,8,48,256]{3,2,1,0:T(8,128)(2,1)S(1)}, bf16[2,8,48,256]{3,2,1,0:T(8,128)(2,1)}, u32[]{:S(2)}) copy-start(bf16[2,8,48,256]{3,2,1,0:T(8,128)(2,1)} %param.5) | copy-start | bytes 1179652
  142.7 24.8 %slice-start = ((s8[10616832]{0:T(1024)(128)(4,1)}), s8[2228224]{0:T(1024)(128)(4,1)S(1)}, s32[]{:S(2)}) async-start(s8[10616832]{0:T(1024)(128)(4,1)} %bitcast.210), calls=%async_computation.7 | async-start | bytes 4456448
  157.4 10.1 %slice-start.1 = ((s8[10616832]{0:T(1024)(128)(4,1)}), s8[4194304]{0:T(1024)(128)(4,1)S(1)}, s32[]{:S(2)}) async-start(s8[10616832]{0:T(1024)(128)(4,1)} %bitcast.210), calls=%async_computation.8 | async-start | bytes 8388608
  157.4 10.1 %slice-start.2 = ((s8[10616832]{0:T(1024)(128)(4,1)}), s8[4194304]{0:T(1024)(128)(4,1)S(1)}, s32[]{:S(2)}) async-start(s8[10616832]{0:T(1024)(128)(4,1)} %bitcast.210), calls=%async_computation.9 | async-start | bytes 8388608
  166.2 5.9 %collective-permute-start.6 = (bf16[2,8,48,256]{3,2,1,0:T(8,128)(2,1)S(1)}, bf16[2,8,48,256]{3,2,1,0:T(8,128)(2,1)S(1)}, u32[]{:S(2)}, u32[]{:S(2)}) collective-permute-start(bf16[2,8,48,256]{3,2,1,0:T(8,128)(2,1)S(1)} %bitcast.232), channel_id=1, source_target_pairs={{16,0},{17,1},{18,2},{19,3},{20,4},{21,5},{22,6},{23,7},{24,8},{25... | collective-permute-start | bytes 1179656 | tf_op jit(solution)/shard_map/ppermute | solution.py:11
  172.1 273.7 %reduce-scatter.3.cloned.1.call-start = ((), (), s32[]{:S(2)}) async-start(), calls=%async_computation.4 | async-start | bytes 3760128 | tf_op jit(solution)/shard_map/reduce_scatter | solution.py:82
  172.2 6.3 %collective-permute-start.7 = (bf16[4,1,48,256]{3,2,1,0:T(8,128)(2,1)S(1)}, bf16[4,1,48,256]{3,2,1,0:T(8,128)(2,1)S(1)}, u32[]{:S(2)}, u32[]{:S(2)}) collective-permute-start(bf16[4,1,48,256]{3,2,1,0:T(8,128)(2,1)S(1)} %get-tuple-element.32), channel_id=1, source_target_pairs={{0,1},{1,2},{2,3},{3,4},{4,5},{5,6},{6,7},{7,8},{8,9},{9,10},{10,1... | collective-permute-start | bytes 294920 | tf_op jit(solution)/shard_map/ppermute | solution.py:22
  175.5 9.0 %collective-permute-start.8 = (bf16[4,1,48,256]{3,2,1,0:T(8,128)(2,1)S(1)}, bf16[4,1,48,256]{3,2,1,0:T(8,128)(2,1)S(1)}, u32[]{:S(2)}, u32[]{:S(2)}) collective-permute-start(bf16[4,1,48,256]{3,2,1,0:T(8,128)(2,1)S(1)} %get-tuple-element.33), channel_id=1, source_target_pairs={{1,0},{2,1},{3,2},{4,3},{5,4},{6,5},{7,6},{8,7},{9,8},{10,9},{11,1... | collective-permute-start | bytes 294920 | tf_op jit(solution)/shard_map/ppermute | solution.py:24
  190.6 19.6 %copy-start.1 = (bf16[6912,256]{1,0:T(8,128)(2,1)S(1)}, bf16[6912,256]{1,0:T(8,128)(2,1)}, u32[]{:S(2)}) copy-start(bf16[6912,256]{1,0:T(8,128)(2,1)} %all-gather.5.cloned.1.call-done) | copy-start | bytes 10616836
  230.6 235.0 %all-reduce.6.cloned.1.call-start = ((), (), s32[]{:S(2)}) async-start(), calls=%async_computation.6 | async-start | bytes 884736 | tf_op jit(solution)/shard_map/psum | solution.py:85
Sparse Core Ops, SparseCore 0:
  10.8 73.6 all-gather.2
  87.3 70.1 all-gather.4
  172.2 134.3 reduce-scatter.4
  311.5 134.1 reduce-scatter.2
  448.0 17.5 all-reduce.5
where the time goes:
time: 476 us
  waiting for transfers between devices  295 us (62%)
  local copies, waits for them, and re-layouts  99.1 us (21%)
  matrix products  42.5 us (9%)
  starting transfers between devices  20.4 us (4%)
  between operations  14.3 us (3%)
    reduce_scatter x2, waiting for transfers between devices, reduce_grad(): lax.psum_scatter(local_grad.astype(jnp.bfloat16), 'height', scatter_dimen...  215 us
    another operation x4, local copies, waits for them, and re-layouts, causal_patches(): jnp.stack(pieces, axis=3).reshape(frames_n * height_n * width_n, 27 * chans)  47.9 us
    unnamed x93, local copies, waits for them, and re-layouts  45.1 us
    all_gather x1, waiting for transfers between devices, shards(): full_one = lax.all_gather(kernel_one, 'height', axis=0, tiled=True)  23.9 us
    dot_general x1, matrix products, shards(): lax.dot_general(patches_clip, grad_pre, contract_rows, preferred_element_...  20.4 us
    psum x1, waiting for transfers between devices, reduce_grad(): return lax.psum(owned, 'tm').astype(jnp.float32)  19.8 us
    all_gather x1, waiting for transfers between devices, shards(): full_two = lax.all_gather(kernel_two, 'height', axis=0, tiled=True)  14.7 us
    ppermute x3, waiting for transfers between devices, extended_2(): lax.ppermute(head, axis, [((i + 1) % count, i) for i in range(ends)])  14.3 us
  transfers between devices with their start and end apart: 14, of which 13 were waited for; matrix products, arithmetic and copies ran while one was open for 28% of the time, Pallas kernels for 0%

commit v1 on v0

--- a/solution.py
+++ b/solution.py
@@ -3,6 +3,12 @@
 import jax.numpy as jnp
 from jax import lax
 from jax.sharding import PartitionSpec as P
+
+
+def joined_along(pieces, dim):
+    pieces = jnp.moveaxis(pieces, 0, dim)
+    lengths = pieces.shape
+    return pieces.reshape(*lengths[:dim], lengths[dim] * lengths[dim + 1], *lengths[dim + 2 :])
 
 
 def shifted(value, axis, by):
@@ -87,7 +93,19 @@
 
 def shards(clip, teacher, kernel_one, kernel_two):
     frames_n, height_n, width_n, chans = clip.shape
-    full_one = lax.all_gather(kernel_one, "height", axis=0, tiled=True)
+    size = lax.axis_size("height")
+    pairs_2 = [(i_2, (i_2 + 1) % size) for i_2 in range(size)]
+    back = [(b, a) for a, b in pairs_2]
+    lower, upper = ([], [])
+    for step in range(size - 1):
+        if step % 2 == 0:
+            lower.append(lax.ppermute(lower[-1] if lower else kernel_one, "height", pairs_2))
+        else:
+            upper.append(lax.ppermute(upper[-1] if upper else kernel_one, "height", back))
+    tiles = jnp.stack([*lower[::-1], kernel_one, *upper])
+    shift = lax.axis_index("height") - len(lower)
+    tiles = tiles[(jnp.arange(size) - shift) % size]
+    full_one = joined_along(tiles, 0)
     patches_clip = causal_patches(clip)
     pre_act = jnp.dot(patches_clip, full_one, preferred_element_type=jnp.float32)
     hidden = jax.nn.silu(pre_act).astype(jnp.bfloat16)

time: 476 us -> 528 us (1.11)
  starting transfers between devices: 20.4 us -> 60.8 us
  waiting for transfers between devices: 295 us -> 303 us
    ppermute x0 -> x15, waiting for transfers between devices: none -> 52.5 us  [the longest x8 44.2 us: shards(): lax.ppermute(lower[-1] if lower else kernel_one, 'height', pairs_2)]
    ppermute x0 -> x15, starting transfers between devices: none -> 42.1 us  [the longest x7 30.8 us: shards(): lax.ppermute(upper[-1] if upper else kernel_one, 'height', back)]
    all_gather x1 -> x0, waiting for transfers between devices: 23.9 us -> none  [shards(): full_one = lax.all_gather(kernel_one, 'height', axis=0, tiled=True)]
    all_gather x1, waiting for transfers between devices: 14.7 us -> 0.01 us  [shards(): full_two = lax.all_gather(kernel_two, 'height', axis=0, tiled=True)]
    ppermute x3, waiting for transfers between devices: 14.3 us -> 8.75 us  [extended_2(): lax.ppermute(head, axis, [((i + 1) % count, i) for i in range(ends)])]
    unnamed x93 -> x118, local copies, waits for them, and re-layouts: 45.1 us -> 45.5 us
  transfers between devices with their start and end apart: 14 -> 28, of which waited for: 13 -> 20; matrix products, arithmetic and copies ran while one was open for 28% -> 26% of each run, Pallas kernels for 0% -> 0%
where the time goes in v1:
time: 528 us; the launch traced here: 527 us
  waiting for transfers between devices  303 us (57%)
  local copies, waits for them, and re-layouts  102 us (19%)
  starting transfers between devices  60.8 us (12%)
  matrix products  42.4 us (8%)
  between operations  14.6 us (3%)
    reduce_scatter x2, waiting for transfers between devices, reduce_grad(): lax.psum_scatter(local_grad.astype(jnp.bfloat16), 'height', scatter_dimen...  218 us
    another operation x4, local copies, waits for them, and re-layouts, causal_patches(): jnp.stack(pieces, axis=3).reshape(frames_n * height_n * width_n, 27 * chans)  47.9 us
    unnamed x118, local copies, waits for them, and re-layouts  45.5 us
    ppermute x8, waiting for transfers between devices, shards(): lax.ppermute(lower[-1] if lower else kernel_one, 'height', pairs_2)  44.2 us
    ppermute x7, starting transfers between devices, shards(): lax.ppermute(upper[-1] if upper else kernel_one, 'height', back)  30.8 us
    dot_general x1, matrix products, shards(): lax.dot_general(patches_clip, grad_pre, contract_rows, preferred_element_...  20.3 us
    psum x1, waiting for transfers between devices, reduce_grad(): return lax.psum(owned, 'tm').astype(jnp.float32)  19.8 us
    ppermute x8, starting transfers between devices, shards(): lax.ppermute(lower[-1] if lower else kernel_one, 'height', pairs_2)  11.3 us
  transfers between devices with their start and end apart: 28, of which 20 were waited for; matrix products, arithmetic and copies ran while one was open for 26% of the time, Pallas kernels for 0%

profile of v1, /device:TPU:0, one launch (start us, length us, event | category | flops | bytes accessed | tf_op | source)
XLA Modules:
  0.0 527.2 jit_solution(3432322773522989440)
XLA Ops:
  12.0 4.1 collective-permute-start.11
  16.2 5.9 %collective-permute-done.3 = bf16[432,256]{1,0:T(8,128)(2,1)S(1)} collective-permute-done((bf16[432,256]{1,0:T(8,128)(2,1)}, bf16[432,256]{1,0:T(8,128)(2,1)S(1)}, u32[]{:S(2)}, u32[]{:S(2)}) %collective-permute-start.3) | collective-permute-done | bytes 221216 | tf_op jit(solution)/shard_map/ppermute | solution.py:102
  24.7 4.9 collective-permute-start.12
  36.7 6.1 %collective-permute-start.13 = (bf16[432,256]{1,0:T(8,128)(2,1)S(1)}, bf16[432,256]{1,0:T(8,128)(2,1)S(1)}, u32[]{:S(2)}, u32[]{:S(2)}) collective-permute-start(bf16[432,256]{1,0:T(8,128)(2,1)S(1)} %collective-permute-done.12), channel_id=1, source_target_pairs={{1,0},{2,1},{3,2},{4,3},{5,4},{6,5},{7,6},{8,7},{9,8},{10,9},{11,1... | collective-permute-start | bytes 663560 | tf_op jit(solution)/shard_map/ppermute | solution.py:104
  44.7 4.6 collective-permute-done.5
  49.3 2.5 collective-permute-start.6
  51.8 8.4 %collective-permute-done.6 = bf16[432,256]{1,0:T(8,128)(2,1)S(1)} collective-permute-done((bf16[432,256]{1,0:T(8,128)(2,1)S(1)}, bf16[432,256]{1,0:T(8,128)(2,1)S(1)}, u32[]{:S(2)}, u32[]{:S(2)}) %collective-permute-start.6) | collective-permute-done | bytes 221216 | tf_op jit(solution)/shard_map/ppermute | solution.py:102
  60.5 5.7 %collective-permute-start.14 = (bf16[432,256]{1,0:T(8,128)(2,1)S(1)}, bf16[432,256]{1,0:T(8,128)(2,1)S(1)}, u32[]{:S(2)}, u32[]{:S(2)}) collective-permute-start(bf16[432,256]{1,0:T(8,128)(2,1)S(1)} %collective-permute-done.13), channel_id=1, source_target_pairs={{1,0},{2,1},{3,2},{4,3},{5,4},{6,5},{7,6},{8,7},{9,8},{10,9},{11,1... | collective-permute-start | bytes 663560 | tf_op jit(solution)/shard_map/ppermute | solution.py:104
  66.2 5.5 %collective-permute-done.7 = bf16[432,256]{1,0:T(8,128)(2,1)S(1)} collective-permute-done((bf16[432,256]{1,0:T(8,128)(2,1)S(1)}, bf16[432,256]{1,0:T(8,128)(2,1)S(1)}, u32[]{:S(2)}, u32[]{:S(2)}) %collective-permute-start.7) | collective-permute-done | bytes 221216 | tf_op jit(solution)/shard_map/ppermute | solution.py:102
  72.9 4.5 collective-permute-start.15
  77.4 10.0 %collective-permute-done.8 = bf16[432,256]{1,0:T(8,128)(2,1)S(1)} collective-permute-done((bf16[432,256]{1,0:T(8,128)(2,1)S(1)}, bf16[432,256]{1,0:T(8,128)(2,1)S(1)}, u32[]{:S(2)}, u32[]{:S(2)}) %collective-permute-start.8) | collective-permute-done | bytes 221216 | tf_op jit(solution)/shard_map/ppermute | solution.py:102
  87.7 3.2 collective-permute-done.15
  93.3 8.7 %collective-permute-done.9 = bf16[432,256]{1,0:T(8,128)(2,1)S(1)} collective-permute-done((bf16[432,256]{1,0:T(8,128)(2,1)S(1)}, bf16[432,256]{1,0:T(8,128)(2,1)S(1)}, u32[]{:S(2)}, u32[]{:S(2)}) %collective-permute-start.9) | collective-permute-done | bytes 221216 | tf_op jit(solution)/shard_map/ppermute | solution.py:102
  101.9 2.5 collective-permute-start.10
  104.5 23.9 %copy.7 = bf16[2,8,48,27,256]{4,3,2,1,0:T(8,128)(2,1)S(1)} copy(bf16[2,8,48,27,256]{4,2,1,0,3:T(8,128)(2,1)S(1)} %bitcast_dynamic-update-slice_fusion.18) | data formatting | bytes 21233664 | tf_op jit(solution)/shard_map/stack | solution.py:67
  128.4 10.2 %copy.9 = bf16[96,8,27,256]{3,1,2,0:T(8,128)(2,1)} copy(bf16[96,8,27,256]{3,2,1,0:T(8,128)(2,1)S(1)} %bitcast.240) | data formatting | bytes 21233664
  138.6 3.1 collective-permute-start.17
  142.2 3.1 collective-permute-done.17
  145.3 2.6 gather_fusion
  147.9 8.8 %multiply_convert_fusion = (bf16[768,256]{1,0:T(8,128)(2,1)S(1)}, f32[768,256]{1,0:T(8,128)}) fusion(bf16[768,6912]{1,0:T(8,128)(2,1)} %bitcast.242, bf16[6912,256]{1,0:T(8,128)(2,1)} %bitcast.248), kind=kOutput, calls=%fused_computation.17 | convolution fusion | flops 2718892032 | bytes 15335424 | tf_op jit(solution)/shard_map/dot_general | solution.py:110
  164.1 4.1 collective-permute-done.20
  170.9 23.9 %copy.8 = bf16[2,8,48,27,256]{4,3,2,1,0:T(8,128)(2,1)S(1)} copy(bf16[2,8,48,27,256]{4,2,1,0,3:T(8,128)(2,1)S(1)} %bitcast_dynamic-update-slice_fusion) | data formatting | bytes 21233664 | tf_op jit(solution)/shard_map/stack | solution.py:67
  194.8 10.2 %copy.10 = bf16[96,8,27,256]{3,1,2,0:T(8,128)(2,1)} copy(bf16[96,8,27,256]{3,2,1,0:T(8,128)(2,1)S(1)} %bitcast.241) | data formatting | bytes 21233664
  205.1 8.8 %fusion.4 = (bf16[768,256]{1,0:T(8,128)(2,1)S(1)}, bf16[768,256]{1,0:T(8,128)(2,1)}) fusion(bf16[2,8,48,256]{3,2,1,0:T(8,128)(2,1)S(1)} %copy-done.7, bf16[768,6912]{1,0:T(8,128)(2,1)} %bitcast.244, bf16[6912,256]{1,0:T(8,128)(2,1)} %all-gather.2.cloned.1.call-done, bf16[768,256]{1,0:T(8,128)(2,1)S(1)} %bitcast.282), kind=kOutput, calls=%fused_computation.13 | convolution fusion | flops 2719285248 | bytes 15728640 | tf_op jit(solution)/shard_map/dot_general | solution.py:114
  215.2 4.5 convolution_convert_fusion
  219.8 5.7 %collective-permute-start.22 = (bf16[4,1,48,256]{3,2,1,0:T(8,128)(2,1)S(1)}, bf16[4,1,48,256]{3,2,1,0:T(8,128)(2,1)S(1)}, u32[]{:S(2)}, u32[]{:S(2)}) collective-permute-start(bf16[4,1,48,256]{3,2,1,0:T(8,128)(2,1)S(1)} %get-tuple-element.32), channel_id=1, source_target_pairs={{0,1},{1,2},{2,3},{3,4},{4,5},{5,6},{6,7},{7,8},{8,9},{9,10},{10,1... | collective-permute-start | bytes 294920 | tf_op jit(solution)/shard_map/ppermute | solution.py:28
  228.5 4.6 collective-permute-done.23
  235.1 4.0 pad_slice_fusion
  258.8 20.3 %convolution_convert_fusion.1 = bf16[6912,256]{1,0:T(8,128)(2,1)} fusion(bf16[768,6912]{1,0:T(8,128)(2,1)} %bitcast.243, bf16[768,27,256]{2,0,1:T(8,128)(2,1)} %constant_dynamic-update-slice_fusion.2, bf16[27,256,256]{2,1,0:T(8,128)(2,1)S(1)} %bitcast.283, f32[768,256]{1,0:T(8,128)} %get-tuple-element.41), kind=kOutput, calls=%fused_computation.2 | convolution fusion | flops 5439356928 | bytes 29097984 | tf_op jit(solution)/shard_map/dot_general | solution.py:137
  279.2 78.9 %reduce-scatter.5.cloned.1.call-done = bf16[432,256]{1,0:T(8,128)(2,1)} async-done(((bf16[6912,256]{1,0:T(8,128)(2,1)}), bf16[432,256]{1,0:T(8,128)(2,1)}) %reduce-scatter.5.cloned.1.call-update) | async-done | bytes 221200 | tf_op jit(solution)/shard_map/reduce_scatter | solution.py:88
  358.1 139.4 %reduce-scatter.3.cloned.1.call-done = bf16[432,256]{1,0:T(8,128)(2,1)} async-done(((bf16[6912,256]{1,0:T(8,128)(2,1)}), bf16[432,256]{1,0:T(8,128)(2,1)}) %reduce-scatter.3.cloned.1.call-update) | async-done | bytes 221200 | tf_op jit(solution)/shard_map/reduce_scatter | solution.py:88
  497.5 19.8 %all-reduce.6.cloned.1.call-done = (bf16[432,256]{1,0:T(8,128)(2,1)}, bf16[432,256]{1,0:T(8,128)(2,1)}) async-done(((bf16[432,256]{1,0:T(8,128)(2,1)}, bf16[432,256]{1,0:T(8,128)(2,1)}), (bf16[432,256]{1,0:T(8,128)(2,1)}, bf16[432,256]{1,0:T(8,128)(2,1)})) %all-reduce.6.cloned.1.call-update) | async-done | bytes 442384 | tf_op jit(solution)/shard_map/psum | solution.py:91
  (172 shorter events, 60.3 us)
Async XLA Ops:
  7.2 197.9 %all-gather.2.cloned.1.call-start = ((), (), s32[]{:S(2)}) async-start(), calls=%async_computation.2 | async-start | bytes 3760128 | tf_op jit(solution)/shard_map/all_gather | solution.py:112
  7.2 22.4 %collective-permute-start = (bf16[2,8,48,256]{3,2,1,0:T(8,128)(2,1)}, bf16[2,8,48,256]{3,2,1,0:T(8,128)(2,1)S(1)}, u32[]{:S(2)}, u32[]{:S(2)}) collective-permute-start(bf16[2,8,48,256]{3,2,1,0:T(8,128)(2,1)} %param.4), channel_id=1, source_target_pairs={{0,16},{1,17},{2,18},{3,19},{4,20},{5,21},{6,22},{7,23},{8,24},{9,... | collective-permute-start | bytes 1179656 | tf_op jit(solution)/shard_map/ppermute | solution.py:17
  9.6 12.5 %collective-permute-start.3 = (bf16[432,256]{1,0:T(8,128)(2,1)}, bf16[432,256]{1,0:T(8,128)(2,1)S(1)}, u32[]{:S(2)}, u32[]{:S(2)}) collective-permute-start(bf16[432,256]{1,0:T(8,128)(2,1)} %param.6), channel_id=1, source_target_pairs={{0,1},{1,2},{2,3},{3,4},{4,5},{5,6},{6,7},{7,8},{8,9},{9,10},{10,1... | collective-permute-start | bytes 663560 | tf_op jit(solution)/shard_map/ppermute | solution.py:102
  12.0 12.7 %collective-permute-start.11 = (bf16[432,256]{1,0:T(8,128)(2,1)}, bf16[432,256]{1,0:T(8,128)(2,1)S(1)}, u32[]{:S(2)}, u32[]{:S(2)}) collective-permute-start(bf16[432,256]{1,0:T(8,128)(2,1)} %param.6), channel_id=1, source_target_pairs={{1,0},{2,1},{3,2},{4,3},{5,4},{6,5},{7,6},{8,7},{9,8},{10,9},{11,1... | collective-permute-start | bytes 663560 | tf_op jit(solution)/shard_map/ppermute | solution.py:104
  16.1 342.0 %reduce-scatter.5.cloned.1.call-start = ((), (), s32[]{:S(2)}) async-start(), calls=%async_computation.4 | async-start | bytes 3760128 | tf_op jit(solution)/shard_map/reduce_scatter | solution.py:88
  22.1 22.2 %copy-start.4 = (bf16[432,256]{1,0:T(8,128)(2,1)}, bf16[432,256]{1,0:T(8,128)(2,1)S(1)}, u32[]{:S(2)}) copy-start(bf16[432,256]{1,0:T(8,128)(2,1)S(1)} %collective-permute-done.3) | copy-start | bytes 663556
  22.1 12.4 %collective-permute-start.4 = (bf16[432,256]{1,0:T(8,128)(2,1)S(1)}, bf16[432,256]{1,0:T(8,128)(2,1)S(1)}, u32[]{:S(2)}, u32[]{:S(2)}) collective-permute-start(bf16[432,256]{1,0:T(8,128)(2,1)S(1)} %collective-permute-done.3), channel_id=1, source_target_pairs={{0,1},{1,2},{2,3},{3,4},{4,5},{5,6},{6,7},{7,8},{8,9},{9,10},{10,1... | collective-permute-start | bytes 663560 | tf_op jit(solution)/shard_map/ppermute | solution.py:102
  24.7 19.6 %copy-start.2 = (bf16[432,256]{1,0:T(8,128)(2,1)}, bf16[432,256]{1,0:T(8,128)(2,1)S(1)}, u32[]{:S(2)}) copy-start(bf16[432,256]{1,0:T(8,128)(2,1)S(1)} %collective-permute-done.11) | copy-start | bytes 663556
  24.7 11.9 %collective-permute-start.12 = (bf16[432,256]{1,0:T(8,128)(2,1)S(1)}, bf16[432,256]{1,0:T(8,128)(2,1)S(1)}, u32[]{:S(2)}, u32[]{:S(2)}) collective-permute-start(bf16[432,256]{1,0:T(8,128)(2,1)S(1)} %collective-permute-done.11), channel_id=1, source_target_pairs={{1,0},{2,1},{3,2},{4,3},{5,4},{6,5},{7,6},{8,7},{9,8},{10,9},{11,1... | collective-permute-start | bytes 663560 | tf_op jit(solution)/shard_map/ppermute | solution.py:104
  30.7 12.0 %collective-permute-start.1 = (bf16[4,1,48,256]{3,2,1,0:T(8,128)(2,1)S(1)}, bf16[4,1,48,256]{3,2,1,0:T(8,128)(2,1)S(1)}, u32[]{:S(2)}, u32[]{:S(2)}) collective-permute-start(bf16[4,1,48,256]{3,2,1,0:T(8,128)(2,1)S(1)} %get-tuple-element.38), channel_id=1, source_target_pairs={{0,1},{1,2},{2,3},{3,4},{4,5},{5,6},{6,7},{7,8},{8,9},{9,10},{10,1... | collective-permute-start | bytes 294920 | tf_op jit(solution)/shard_map/ppermute | solution.py:28
  32.0 10.7 %collective-permute-start.2 = (bf16[4,1,48,256]{3,2,1,0:T(8,128)(2,1)S(1)}, bf16[4,1,48,256]{3,2,1,0:T(8,128)(2,1)S(1)}, u32[]{:S(2)}, u32[]{:S(2)}) collective-permute-start(bf16[4,1,48,256]{3,2,1,0:T(8,128)(2,1)S(1)} %get-tuple-element.39), channel_id=1, source_target_pairs={{1,0},{2,1},{3,2},{4,3},{5,4},{6,5},{7,6},{8,7},{9,8},{10,9},{11,1... | collective-permute-start | bytes 294920 | tf_op jit(solution)/shard_map/ppermute | solution.py:30
  34.5 14.8 %collective-permute-start.5 = (bf16[432,256]{1,0:T(8,128)(2,1)S(1)}, bf16[432,256]{1,0:T(8,128)(2,1)S(1)}, u32[]{:S(2)}, u32[]{:S(2)}) collective-permute-start(bf16[432,256]{1,0:T(8,128)(2,1)S(1)} %collective-permute-done.4), channel_id=1, source_target_pairs={{0,1},{1,2},{2,3},{3,4},{4,5},{5,6},{6,7},{7,8},{8,9},{9,10},{10,1... | collective-permute-start | bytes 663560 | tf_op jit(solution)/shard_map/ppermute | solution.py:102
  36.7 23.8 %collective-permute-start.13 = (bf16[432,256]{1,0:T(8,128)(2,1)S(1)}, bf16[432,256]{1,0:T(8,128)(2,1)S(1)}, u32[]{:S(2)}, u32[]{:S(2)}) collective-permute-start(bf16[432,256]{1,0:T(8,128)(2,1)S(1)} %collective-permute-done.12), channel_id=1, source_target_pairs={{1,0},{2,1},{3,2},{4,3},{5,4},{6,5},{7,6},{8,7},{9,8},{10,9},{11,1... | collective-permute-start | bytes 663560 | tf_op jit(solution)/shard_map/ppermute | solution.py:104
  49.3 10.9 %collective-permute-start.6 = (bf16[432,256]{1,0:T(8,128)(2,1)S(1)}, bf16[432,256]{1,0:T(8,128)(2,1)S(1)}, u32[]{:S(2)}, u32[]{:S(2)}) collective-permute-start(bf16[432,256]{1,0:T(8,128)(2,1)S(1)} %collective-permute-done.5), channel_id=1, source_target_pairs={{0,1},{1,2},{2,3},{3,4},{4,5},{5,6},{6,7},{7,8},{8,9},{9,10},{10,1... | collective-permute-start | bytes 663560 | tf_op jit(solution)/shard_map/ppermute | solution.py:102
  60.3 11.4 %collective-permute-start.7 = (bf16[432,256]{1,0:T(8,128)(2,1)S(1)}, bf16[432,256]{1,0:T(8,128)(2,1)S(1)}, u32[]{:S(2)}, u32[]{:S(2)}) collective-permute-start(bf16[432,256]{1,0:T(8,128)(2,1)S(1)} %collective-permute-done.6), channel_id=1, source_target_pairs={{0,1},{1,2},{2,3},{3,4},{4,5},{5,6},{6,7},{7,8},{8,9},{9,10},{10,1... | collective-permute-start | bytes 663560 | tf_op jit(solution)/shard_map/ppermute | solution.py:102
  60.5 12.4 %collective-permute-start.14 = (bf16[432,256]{1,0:T(8,128)(2,1)S(1)}, bf16[432,256]{1,0:T(8,128)(2,1)S(1)}, u32[]{:S(2)}, u32[]{:S(2)}) collective-permute-start(bf16[432,256]{1,0:T(8,128)(2,1)S(1)} %collective-permute-done.13), channel_id=1, source_target_pairs={{1,0},{2,1},{3,2},{4,3},{5,4},{6,5},{7,6},{8,7},{9,8},{10,9},{11,1... | collective-permute-start | bytes 663560 | tf_op jit(solution)/shard_map/ppermute | solution.py:104
  71.7 15.7 %collective-permute-start.8 = (bf16[432,256]{1,0:T(8,128)(2,1)S(1)}, bf16[432,256]{1,0:T(8,128)(2,1)S(1)}, u32[]{:S(2)}, u32[]{:S(2)}) collective-permute-start(bf16[432,256]{1,0:T(8,128)(2,1)S(1)} %collective-permute-done.7), channel_id=1, source_target_pairs={{0,1},{1,2},{2,3},{3,4},{4,5},{5,6},{6,7},{7,8},{8,9},{9,10},{10,1... | collective-permute-start | bytes 663560 | tf_op jit(solution)/shard_map/ppermute | solution.py:102
  72.9 18.0 %collective-permute-start.15 = (bf16[432,256]{1,0:T(8,128)(2,1)S(1)}, bf16[432,256]{1,0:T(8,128)(2,1)S(1)}, u32[]{:S(2)}, u32[]{:S(2)}) collective-permute-start(bf16[432,256]{1,0:T(8,128)(2,1)S(1)} %collective-permute-done.14), channel_id=1, source_target_pairs={{1,0},{2,1},{3,2},{4,3},{5,4},{6,5},{7,6},{8,7},{9,8},{10,9},{11,1... | collective-permute-start | bytes 663560 | tf_op jit(solution)/shard_map/ppermute | solution.py:104
  87.4 14.6 %collective-permute-start.9 = (bf16[432,256]{1,0:T(8,128)(2,1)S(1)}, bf16[432,256]{1,0:T(8,128)(2,1)S(1)}, u32[]{:S(2)}, u32[]{:S(2)}) collective-permute-start(bf16[432,256]{1,0:T(8,128)(2,1)S(1)} %collective-permute-done.8), channel_id=1, source_target_pairs={{0,1},{1,2},{2,3},{3,4},{4,5},{5,6},{6,7},{7,8},{8,9},{9,10},{10,1... | collective-permute-start | bytes 663560 | tf_op jit(solution)/shard_map/ppermute | solution.py:102
  90.8 47.8 %collective-permute-start.16 = (bf16[432,256]{1,0:T(8,128)(2,1)S(1)}, bf16[432,256]{1,0:T(8,128)(2,1)S(1)}, u32[]{:S(2)}, u32[]{:S(2)}) collective-permute-start(bf16[432,256]{1,0:T(8,128)(2,1)S(1)} %collective-permute-done.15), channel_id=1, source_target_pairs={{1,0},{2,1},{3,2},{4,3},{5,4},{6,5},{7,6},{8,7},{9,8},{10,9},{11,1... | collective-permute-start | bytes 663560 | tf_op jit(solution)/shard_map/ppermute | solution.py:104
  101.9 39.9 %collective-permute-start.10 = (bf16[432,256]{1,0:T(8,128)(2,1)S(1)}, bf16[432,256]{1,0:T(8,128)(2,1)S(1)}, u32[]{:S(2)}, u32[]{:S(2)}) collective-permute-start(bf16[432,256]{1,0:T(8,128)(2,1)S(1)} %collective-permute-done.9), channel_id=1, source_target_pairs={{0,1},{1,2},{2,3},{3,4},{4,5},{5,6},{6,7},{7,8},{8,9},{9,10},{10,1... | collective-permute-start | bytes 663560 | tf_op jit(solution)/shard_map/ppermute | solution.py:102
  128.4 13.6 %copy-start.3 = (bf16[432,256]{1,0:T(8,128)(2,1)S(1)}, bf16[432,256]{1,0:T(8,128)(2,1)}, u32[]{:S(2)}) copy-start(bf16[432,256]{1,0:T(8,128)(2,1)} %copy-done.2) | copy-start | bytes 663556
  138.6 6.6 %collective-permute-start.17 = (bf16[432,256]{1,0:T(8,128)(2,1)S(1)}, bf16[432,256]{1,0:T(8,128)(2,1)S(1)}, u32[]{:S(2)}, u32[]{:S(2)}) collective-permute-start(bf16[432,256]{1,0:T(8,128)(2,1)S(1)} %collective-permute-done.16), channel_id=1, source_target_pairs={{1,0},{2,1},{3,2},{4,3},{5,4},{6,5},{7,6},{8,7},{9,8},{10,9},{11,1... | collective-permute-start | bytes 663560 | tf_op jit(solution)/shard_map/ppermute | solution.py:104
  156.7 2.6 collective-permute-start.18
  159.4 4.7 collective-permute-start.19
  161.5 6.7 %collective-permute-start.20 = (bf16[4,1,48,256]{3,2,1,0:T(8,128)(2,1)S(1)}, bf16[4,1,48,256]{3,2,1,0:T(8,128)(2,1)S(1)}, u32[]{:S(2)}, u32[]{:S(2)}) collective-permute-start(bf16[4,1,48,256]{3,2,1,0:T(8,128)(2,1)S(1)} %get-tuple-element.37), channel_id=1, source_target_pairs={{1,0},{2,1},{3,2},{4,3},{5,4},{6,5},{7,6},{8,7},{9,8},{10,9},{11,1... | collective-permute-start | bytes 294920 | tf_op jit(solution)/shard_map/ppermute | solution.py:30
  213.9 5.9 %collective-permute-start.21 = (bf16[2,8,48,256]{3,2,1,0:T(8,128)(2,1)S(1)}, bf16[2,8,48,256]{3,2,1,0:T(8,128)(2,1)S(1)}, u32[]{:S(2)}, u32[]{:S(2)}) collective-permute-start(bf16[2,8,48,256]{3,2,1,0:T(8,128)(2,1)S(1)} %bitcast.268), channel_id=1, source_target_pairs={{16,0},{17,1},{18,2},{19,3},{20,4},{21,5},{22,6},{23,7},{24,8},{25... | collective-permute-start | bytes 1179656 | tf_op jit(solution)/shard_map/ppermute | solution.py:17
  219.7 277.8 %reduce-scatter.3.cloned.1.call-start = ((), (), s32[]{:S(2)}) async-start(), calls=%async_computation.3 | async-start | bytes 3760128 | tf_op jit(solution)/shard_map/reduce_scatter | solution.py:88
  219.8 8.7 %collective-permute-start.22 = (bf16[4,1,48,256]{3,2,1,0:T(8,128)(2,1)S(1)}, bf16[4,1,48,256]{3,2,1,0:T(8,128)(2,1)S(1)}, u32[]{:S(2)}, u32[]{:S(2)}) collective-permute-start(bf16[4,1,48,256]{3,2,1,0:T(8,128)(2,1)S(1)} %get-tuple-element.32), channel_id=1, source_target_pairs={{0,1},{1,2},{2,3},{3,4},{4,5},{5,6},{6,7},{7,8},{8,9},{9,10},{10,1... | collective-permute-start | bytes 294920 | tf_op jit(solution)/shard_map/ppermute | solution.py:28
  225.5 7.6 %collective-permute-start.23 = (bf16[4,1,48,256]{3,2,1,0:T(8,128)(2,1)S(1)}, bf16[4,1,48,256]{3,2,1,0:T(8,128)(2,1)S(1)}, u32[]{:S(2)}, u32[]{:S(2)}) collective-permute-start(bf16[4,1,48,256]{3,2,1,0:T(8,128)(2,1)S(1)} %get-tuple-element.33), channel_id=1, source_target_pairs={{1,0},{2,1},{3,2},{4,3},{5,4},{6,5},{7,6},{8,7},{9,8},{10,9},{11,1... | collective-permute-start | bytes 294920 | tf_op jit(solution)/shard_map/ppermute | solution.py:30
  239.2 19.6 %copy-start.6 = (bf16[6912,256]{1,0:T(8,128)(2,1)S(1)}, bf16[6912,256]{1,0:T(8,128)(2,1)}, u32[]{:S(2)}) copy-start(bf16[6912,256]{1,0:T(8,128)(2,1)} %all-gather.2.cloned.1.call-done) | copy-start | bytes 10616836
  279.1 238.1 %all-reduce.6.cloned.1.call-start = ((), (), s32[]{:S(2)}) async-start(), calls=%async_computation.5 | async-start | bytes 884736 | tf_op jit(solution)/shard_map/psum | solution.py:91
  (7 other events, 78.1 us)
Sparse Core Ops, SparseCore 0:
  16.2 92.7 all-gather.1
  219.8 138.2 reduce-scatter.4
  363.2 134.2 reduce-scatter.2
  499.7 17.4 all-reduce.5
